TPU v7x, 32 devices: a whole 2x2x4 slice. The times are simulated.
32 devices in a mesh: grp: 2 (over x), lon: 16 (over z, y, core).
Axes of the slice: x: 2, y: 2, z: 4, core: 2. Of those that a mesh axis runs over, the one named last changes fastest.
Arguments:
- tracer_pert: float32 [4, 50, 32, 1024], P('grp', None, 'lon'), parts along dimension 0, may hold values from -60 to 60
- surface_pert: float32 [4, 32, 1024], P('grp', 'lon'), parts along dimension 0, may hold values from -60 to 60
- zonal_flow: float32 [50, 32, 1024], P(None, 'lon'), may hold values from -3.2 to 3.2
- merid_flow: float32 [50, 32, 1024], P(None, 'lon'), may hold values from -3.2 to 3.2
- bottom_level: int32 [32, 1024], P('lon'), may hold values from 0 to 50
Outputs:
- tracer_vec: float32 [4, 50, 32, 1024], P('grp', None, 'lon'), parts along dimension 0
- surface_vec: float32 [4, 32, 1024], P('grp', 'lon'), parts along dimension 0
- growth: float32 [6], P('grp'), parts along dimension 0
There are 2 independent parts, one for each index of `grp`. A program takes and returns all parts, laid end to end along the dimension named above; an argument that names none is the same for every part. Nothing has to cross between parts.
Inputs may be any that keep to these rules, and one draw needn't show every extreme that they name: `bottom_level`: 0 marks a land column, 50 a column wet to the bottom level.
All inputs are finite; a program needn't handle non-finite values.
Results may differ from a plain program's by a relative error of at most 0.0001.
Values sent between devices are 32-bit elements; how exact they have to be, the bound alone decides.
A program may use at most 64 MiB of HBM per device.

v0:
```python
import jax
import jax.numpy as jnp
from jax import lax
from jax.sharding import PartitionSpec as P

ITERS = 3
DIFFUSIVITY = 0.5
TIME_STEP = 0.2
SURFACE_COUPLING = 0.5
STERIC_GAIN = 2.0
EPSILON = 1e-06


def extended_2(block, sides, width):
    for axis, dim in sides:
        count = lax.axis_size(axis)
        forward = [(i, i + 1) for i in range(count - 1)]
        forward.append((count - 1, 0))
        backward = [(target, source) for source, target in forward]
        low = lax.ppermute(
            lax.slice_in_dim(block, block.shape[dim] - width, None, axis=dim), axis, forward
        )
        high = lax.ppermute(lax.slice_in_dim(block, 0, width, axis=dim), axis, backward)
        block = jnp.concatenate([low, block, high], axis=dim)
    return block


def tracer_update(tracer, zonal_flow, merid_flow, wet_cells):
    face_x = wet_cells[:, :-1] * wet_cells[:, 1:]
    flow_x = 0.5 * (zonal_flow[:, :-1] + zonal_flow[:, 1:])
    west_vals = tracer[:, :, :-1]
    east_vals = tracer[:, :, 1:]
    flux_x = face_x * (
        0.5 * flow_x * (west_vals + east_vals) - DIFFUSIVITY * (east_vals - west_vals)
    )
    div_x = flux_x[:, :, 1:] - flux_x[:, :, :-1]
    interior = tracer[:, :, 1:-1]
    wet_mid = wet_cells[:, 1:-1]
    merid_mid = merid_flow[:, 1:-1]
    face_y = wet_mid[..., :-1] * wet_mid[..., 1:]
    flow_y = 0.5 * (merid_mid[..., :-1] + merid_mid[..., 1:])
    flux_y = face_y * (
        0.5 * flow_y * (interior[..., :-1] + interior[..., 1:])
        - DIFFUSIVITY * (interior[..., 1:] - interior[..., :-1])
    )
    padded = jnp.pad(flux_y, ((0, 0), (0, 0), (0, 0), (1, 1)))
    div_y = padded[..., 1:] - padded[..., :-1]
    return interior - TIME_STEP * (div_x + div_y)


def surface_operator(extended, face_x, face_y):
    grad_x = face_x * (extended[:, 1:] - extended[:, :-1])
    lap_x = grad_x[:, 1:] - grad_x[:, :-1]
    center = extended[:, 1:-1]
    grad_y = face_y * (center[..., 1:] - center[..., :-1])
    padded = jnp.pad(grad_y, ((0, 0), (0, 0), (1, 1)))
    lap_y = padded[..., 1:] - padded[..., :-1]
    return center - SURFACE_COUPLING * (lap_x + lap_y)


def apply_operator(surface, face_x, face_y):
    extended = extended_2(surface, (("lon", 1),), 1)
    return surface_operator(extended, face_x, face_y)


def local_products(lhs_field, rhs_field):
    return jnp.sum(lhs_field * rhs_field, axis=(1, 2))


def residual_squares(residual):
    return lax.psum(local_products(residual, residual), "lon")


def on_device(tracer_pert, surface_pert, zonal_flow, merid_flow, bottom_level):
    vectors, levels_count, columns, lat_rows = tracer_pert.shape
    levels = jnp.arange(levels_count, dtype=jnp.float32)[:, None, None]
    depths = bottom_level.astype(jnp.float32)
    wet_cells = (levels < depths[None]).astype(jnp.float32)
    tracer = wet_cells[None] * tracer_pert
    lead_rows = vectors * levels_count
    stacked = jnp.concatenate(
        [
            tracer.reshape(lead_rows, columns, lat_rows),
            surface_pert,
            zonal_flow,
            merid_flow,
            depths[None],
        ],
        axis=0,
    )
    extended = extended_2(stacked, (("lon", 1),), 1)
    tracer_ext = extended[:lead_rows].reshape(vectors, levels_count, columns + 2, lat_rows)
    zonal_ext = extended[lead_rows + vectors : lead_rows + vectors + levels_count]
    merid_ext = extended[
        lead_rows + vectors + levels_count : lead_rows + vectors + 2 * levels_count
    ]
    depth_ext = extended[-1]
    wet_ext = (levels < depth_ext[None]).astype(jnp.float32)
    tracer = tracer_update(tracer_ext, zonal_ext, merid_ext, wet_ext)
    refreshed = extended_2(tracer, (("lon", 2),), 1)
    tracer = tracer_update(refreshed, zonal_ext, merid_ext, wet_ext)
    surface_rim = extended[lead_rows : lead_rows + vectors]
    depth_rim = extended[-1]
    land_free = (depth_rim > 0).astype(jnp.float32)
    height_ext = surface_rim * land_free[None]
    face_x = jnp.minimum(depth_rim[:-1], depth_rim[1:])
    depth_mid = depth_rim[1:-1]
    face_y = jnp.minimum(depth_mid[:, :-1], depth_mid[:, 1:])
    height = height_ext[:, 1:-1]
    forcing = height + STERIC_GAIN * jnp.sum(tracer, axis=1) / levels_count
    residual = forcing - surface_operator(height_ext, face_x, face_y)
    solution = height
    direction = residual
    norm_now = residual_squares(residual)
    for iteration in range(ITERS):
        image_vec = apply_operator(direction, face_x, face_y)
        step_size = norm_now / lax.psum(local_products(direction, image_vec), "lon")
        solution = solution + step_size[:, None, None] * direction
        residual = residual - step_size[:, None, None] * image_vec
        if iteration + 1 < ITERS:
            norm_next = residual_squares(residual)
            direction = residual + (norm_next / norm_now)[:, None, None] * direction
            norm_now = norm_next
    cell_count = (levels_count + 1) * columns * lat_rows * lax.axis_size("lon")

    def local_inner(tracer_a, surface_a, tracer_b, surface_b):
        return (jnp.sum(tracer_a * tracer_b) + jnp.sum(surface_a * surface_b)) / cell_count

    first_tracer, second_tracer = (tracer[0], tracer[1])
    first_surface, second_surface = (solution[0], solution[1])
    gram_one, gram_mix, gram_two = lax.psum(
        (
            local_inner(first_tracer, first_surface, first_tracer, first_surface),
            local_inner(second_tracer, second_surface, first_tracer, first_surface),
            local_inner(second_tracer, second_surface, second_tracer, second_surface),
        ),
        "lon",
    )
    scale_one = jnp.sqrt(gram_one + EPSILON)
    cross = gram_mix / scale_one
    unit_tracer = first_tracer / scale_one
    unit_surface = first_surface / scale_one
    rest_tracer = second_tracer - cross * unit_tracer
    rest_surface = second_surface - cross * unit_surface
    rest_norm = gram_two - 2.0 * cross * cross + cross * cross * gram_one / (gram_one + EPSILON)
    scale_two = jnp.sqrt(rest_norm + EPSILON)
    tracer_vec = jnp.stack([unit_tracer, rest_tracer / scale_two])
    surface_vec = jnp.stack([unit_surface, rest_surface / scale_two])
    growth = jnp.stack([scale_one, cross, scale_two])
    return (tracer_vec, surface_vec, growth)


def solution(mesh):
    placed = (
        P("grp", None, "lon", None),
        P("grp", "lon", None),
        P(None, "lon", None),
        P(None, "lon", None),
        P("lon", None),
    )
    return jax.shard_map(
        on_device,
        mesh=mesh,
        in_specs=placed,
        out_specs=(P("grp", None, "lon", None), P("grp", "lon", None), P("grp")),
        check_vma=False,
    )
```

profile of v0, /device:TPU:0, one launch (start us, length us, event | category | flops | bytes accessed | tf_op | source)
XLA Modules:
  0.0 270.8 jit_solution(4647945465952432828)
XLA Ops:
  1.5 1.6 broadcast_multiply_fusion
  4.2 1.3 fusion.35
  5.6 5.5 %collective-permute-start.1 = (f32[203,1,1024]{2,0,1:T(8,128)S(1)}, f32[203,1,1024]{2,0,1:T(8,128)S(1)}, u32[]{:S(2)}, u32[]{:S(2)}) collective-permute-start(f32[203,1,1024]{2,0,1:T(8,128)S(1)} %copy.20), channel_id=1, source_target_pairs={{1,0},{2,1},{3,2},{4,3},{5,4},{6,5},{7,6},{8,7},{9,8},{10,9},{11,1... | collective-permute-start | bytes 2494472 | tf_op jit(solution)/shard_map/ppermute | solution.py:23
  12.1 9.2 %collective-permute-done.1 = f32[203,1,1024]{2,0,1:T(8,128)S(1)} collective-permute-done((f32[203,1,1024]{2,0,1:T(8,128)S(1)}, f32[203,1,1024]{2,0,1:T(8,128)S(1)}, u32[]{:S(2)}, u32[]{:S(2)}) %collective-permute-start.1) | collective-permute-done | bytes 831520 | tf_op jit(solution)/shard_map/ppermute | solution.py:23
  22.2 4.2 %collective-permute-done = f32[203,1,1024]{2,0,1:T(8,128)S(1)} collective-permute-done((f32[203,1,1024]{2,0,1:T(8,128)S(1)}, f32[203,1,1024]{2,0,1:T(8,128)S(1)}, u32[]{:S(2)}, u32[]{:S(2)}) %collective-permute-start) | collective-permute-done | bytes 831520 | tf_op jit(solution)/shard_map/ppermute | solution.py:20
  29.0 2.6 pad_maximum_fusion
  31.7 1.5 subtract_multiply_fusion.3
  34.1 1.5 fusion.5
  36.3 2.8 %collective-permute-start.2 = (f32[2,50,1,1024]{3,2,1,0:T(1,128)S(1)}, f32[2,50,1,1024]{3,2,1,0:T(1,128)S(1)}, u32[]{:S(2)}, u32[]{:S(2)}) collective-permute-start(f32[2,50,1,1024]{3,2,1,0:T(1,128)S(1)} %get-tuple-element.36), channel_id=1, source_target_pairs={{0,1},{1,2},{2,3},{3,4},{4,5},{5,6},{6,7},{7,8},{8,9},{9,10},{10,1... | collective-permute-start | bytes 1228808 | tf_op jit(solution)/shard_map/ppermute | solution.py:20
  39.0 1.7 collective-permute-start.3
  42.0 4.5 %collective-permute-done.2 = f32[2,50,1,1024]{3,2,1,0:T(1,128)S(1)} collective-permute-done((f32[2,50,1,1024]{3,2,1,0:T(1,128)S(1)}, f32[2,50,1,1024]{3,2,1,0:T(1,128)S(1)}, u32[]{:S(2)}, u32[]{:S(2)}) %collective-permute-start.2) | collective-permute-done | bytes 409632 | tf_op jit(solution)/shard_map/ppermute | solution.py:20
  46.5 1.7 subtract_multiply_fusion
  48.3 1.5 fusion.33
  49.9 4.2 %collective-permute-start.5 = (f32[2,1,1024]{2,1,0:T(1,128)S(1)}, f32[2,1,1024]{2,1,0:T(1,128)S(1)}, u32[]{:S(2)}, u32[]{:S(2)}) collective-permute-start(f32[2,1,1024]{2,1,0:T(1,128)S(1)} %get-tuple-element.42), channel_id=1, source_target_pairs={{0,1},{1,2},{2,3},{3,4},{4,5},{5,6},{6,7},{7,8},{8,9},{9,10},{10,1... | collective-permute-start | bytes 24584 | tf_op jit(solution)/shard_map/ppermute | solution.py:20
  56.4 33.5 %all-reduce.7 = (f32[2]{0:T(128)S(1)}, f32[2]{0:T(128)S(1)}) all-reduce(f32[2]{0:T(128)S(1)} %get-tuple-element.13, f32[2]{0:T(128)S(1)} %get-tuple-element.12), channel_id=1, replica_groups=mesh['grp'=2,'lon'=16] {'lon'}, use_global_device_ids=true, to_apply=%region_3.4 | all-reduce | flops 4 | bytes 32 | tf_op jit(solution)/shard_map/psum | solution.py:71
  90.1 29.5 %psum.65 = f32[2]{0:T(128)S(1)} all-reduce(f32[2]{0:T(128)S(1)} %get-tuple-element.27), channel_id=1, replica_groups=mesh['grp'=2,'lon'=16] {'lon'}, use_global_device_ids=true, to_apply=%region_7.8 | all-reduce | flops 2 | bytes 16 | tf_op jit(solution)/shard_map/psum | solution.py:71
  119.8 4.4 %collective-permute-start.6 = (f32[2,1,1024]{2,1,0:T(1,128)S(1)}, f32[2,1,1024]{2,1,0:T(1,128)S(1)}, u32[]{:S(2)}, u32[]{:S(2)}) collective-permute-start(f32[2,1,1024]{2,1,0:T(1,128)S(1)} %get-tuple-element.41), channel_id=1, source_target_pairs={{1,0},{2,1},{3,2},{4,3},{5,4},{6,5},{7,6},{8,7},{9,8},{10,9},{11,1... | collective-permute-start | bytes 24584 | tf_op jit(solution)/shard_map/ppermute | solution.py:23
  124.3 1.2 collective-permute-done.7
  125.8 33.9 %psum.66 = f32[2]{0:T(128)S(1)} all-reduce(f32[2]{0:T(128)S(1)} %get-tuple-element.25), channel_id=1, replica_groups=mesh['grp'=2,'lon'=16] {'lon'}, use_global_device_ids=true, to_apply=%region_9.10 | all-reduce | flops 2 | bytes 16 | tf_op jit(solution)/shard_map/psum | solution.py:117
  159.9 29.5 %psum.67 = f32[2]{0:T(128)S(1)} all-reduce(f32[2]{0:T(128)S(1)} %get-tuple-element.23), channel_id=1, replica_groups=mesh['grp'=2,'lon'=16] {'lon'}, use_global_device_ids=true, to_apply=%region_11.12 | all-reduce | flops 2 | bytes 16 | tf_op jit(solution)/shard_map/psum | solution.py:71
  189.5 4.4 %collective-permute-start.8 = (f32[2,1,1024]{2,1,0:T(1,128)S(1)}, f32[2,1,1024]{2,1,0:T(1,128)S(1)}, u32[]{:S(2)}, u32[]{:S(2)}) collective-permute-start(f32[2,1,1024]{2,1,0:T(1,128)S(1)} %get-tuple-element.39), channel_id=1, source_target_pairs={{1,0},{2,1},{3,2},{4,3},{5,4},{6,5},{7,6},{8,7},{9,8},{10,9},{11,1... | collective-permute-start | bytes 24584 | tf_op jit(solution)/shard_map/ppermute | solution.py:23
  196.8 33.9 %psum.68 = f32[2]{0:T(128)S(1)} all-reduce(f32[2]{0:T(128)S(1)} %fusion.12), channel_id=1, replica_groups=mesh['grp'=2,'lon'=16] {'lon'}, use_global_device_ids=true, to_apply=%region_13.14 | all-reduce | flops 2 | bytes 16 | tf_op jit(solution)/shard_map/psum | solution.py:117
  235.2 30.0 %all-reduce.6 = (f32[]{:T(128)}, f32[]{:T(128)}, f32[]{:T(128)}) all-reduce(f32[]{:T(128)S(6)} %div.73, f32[]{:T(128)S(6)} %div.78, f32[]{:T(128)S(6)} %div.76), channel_id=1, replica_groups=mesh['grp'=2,'lon'=16] {'lon'}, use_global_device_ids=true, to_apply=%region_15.16 | all-reduce | flops 3 | bytes 24 | tf_op jit(solution)/shard_map/psum | solution.py:131
  268.9 1.3 pad_maximum_fusion.3
  (72 shorter events, 17.7 us)
Async XLA Ops:
  1.5 1.7 copy-start.3
  1.5 1.7 copy-start.1
  3.1 1.0 copy-start
  3.1 1.1 copy-start.2
  5.6 15.7 %collective-permute-start.1 = (f32[203,1,1024]{2,0,1:T(8,128)S(1)}, f32[203,1,1024]{2,0,1:T(8,128)S(1)}, u32[]{:S(2)}, u32[]{:S(2)}) collective-permute-start(f32[203,1,1024]{2,0,1:T(8,128)S(1)} %copy.20), channel_id=1, source_target_pairs={{1,0},{2,1},{3,2},{4,3},{5,4},{6,5},{7,6},{8,7},{9,8},{10,9},{11,1... | collective-permute-start | bytes 2494472 | tf_op jit(solution)/shard_map/ppermute | solution.py:23
  11.3 15.1 %collective-permute-start = (f32[203,1,1024]{2,0,1:T(8,128)S(1)}, f32[203,1,1024]{2,0,1:T(8,128)S(1)}, u32[]{:S(2)}, u32[]{:S(2)}) collective-permute-start(f32[203,1,1024]{2,0,1:T(8,128)S(1)} %copy.19), channel_id=1, source_target_pairs={{0,1},{1,2},{2,3},{3,4},{4,5},{5,6},{6,7},{7,8},{8,9},{9,10},{10,1... | collective-permute-start | bytes 2494472 | tf_op jit(solution)/shard_map/ppermute | solution.py:20
  36.3 10.2 %collective-permute-start.2 = (f32[2,50,1,1024]{3,2,1,0:T(1,128)S(1)}, f32[2,50,1,1024]{3,2,1,0:T(1,128)S(1)}, u32[]{:S(2)}, u32[]{:S(2)}) collective-permute-start(f32[2,50,1,1024]{3,2,1,0:T(1,128)S(1)} %get-tuple-element.36), channel_id=1, source_target_pairs={{0,1},{1,2},{2,3},{3,4},{4,5},{5,6},{6,7},{7,8},{8,9},{9,10},{10,1... | collective-permute-start | bytes 1228808 | tf_op jit(solution)/shard_map/ppermute | solution.py:20
  39.0 7.5 %collective-permute-start.3 = (f32[2,50,1,1024]{3,2,1,0:T(1,128)S(1)}, f32[2,50,1,1024]{3,2,1,0:T(1,128)S(1)}, u32[]{:S(2)}, u32[]{:S(2)}) collective-permute-start(f32[2,50,1,1024]{3,2,1,0:T(1,128)S(1)} %get-tuple-element.37), channel_id=1, source_target_pairs={{1,0},{2,1},{3,2},{4,3},{5,4},{6,5},{7,6},{8,7},{9,8},{10,9},{11,1... | collective-permute-start | bytes 1228808 | tf_op jit(solution)/shard_map/ppermute | solution.py:23
  49.9 5.8 %collective-permute-start.5 = (f32[2,1,1024]{2,1,0:T(1,128)S(1)}, f32[2,1,1024]{2,1,0:T(1,128)S(1)}, u32[]{:S(2)}, u32[]{:S(2)}) collective-permute-start(f32[2,1,1024]{2,1,0:T(1,128)S(1)} %get-tuple-element.42), channel_id=1, source_target_pairs={{0,1},{1,2},{2,3},{3,4},{4,5},{5,6},{6,7},{7,8},{8,9},{9,10},{10,1... | collective-permute-start | bytes 24584 | tf_op jit(solution)/shard_map/ppermute | solution.py:20
  54.1 2.1 collective-permute-start.4
  119.7 5.8 %collective-permute-start.7 = (f32[2,1,1024]{2,1,0:T(1,128)S(1)}, f32[2,1,1024]{2,1,0:T(1,128)S(1)}, u32[]{:S(2)}, u32[]{:S(2)}) collective-permute-start(f32[2,1,1024]{2,1,0:T(1,128)S(1)} %get-tuple-element.40), channel_id=1, source_target_pairs={{0,1},{1,2},{2,3},{3,4},{4,5},{5,6},{6,7},{7,8},{8,9},{9,10},{10,1... | collective-permute-start | bytes 24584 | tf_op jit(solution)/shard_map/ppermute | solution.py:20
  119.8 5.8 %collective-permute-start.6 = (f32[2,1,1024]{2,1,0:T(1,128)S(1)}, f32[2,1,1024]{2,1,0:T(1,128)S(1)}, u32[]{:S(2)}, u32[]{:S(2)}) collective-permute-start(f32[2,1,1024]{2,1,0:T(1,128)S(1)} %get-tuple-element.41), channel_id=1, source_target_pairs={{1,0},{2,1},{3,2},{4,3},{5,4},{6,5},{7,6},{8,7},{9,8},{10,9},{11,1... | collective-permute-start | bytes 24584 | tf_op jit(solution)/shard_map/ppermute | solution.py:23
  189.4 5.8 %collective-permute-start.9 = (f32[2,1,1024]{2,1,0:T(1,128)S(1)}, f32[2,1,1024]{2,1,0:T(1,128)S(1)}, u32[]{:S(2)}, u32[]{:S(2)}) collective-permute-start(f32[2,1,1024]{2,1,0:T(1,128)S(1)} %get-tuple-element.38), channel_id=1, source_target_pairs={{0,1},{1,2},{2,3},{3,4},{4,5},{5,6},{6,7},{7,8},{8,9},{9,10},{10,1... | collective-permute-start | bytes 24584 | tf_op jit(solution)/shard_map/ppermute | solution.py:20
  189.5 5.8 %collective-permute-start.8 = (f32[2,1,1024]{2,1,0:T(1,128)S(1)}, f32[2,1,1024]{2,1,0:T(1,128)S(1)}, u32[]{:S(2)}, u32[]{:S(2)}) collective-permute-start(f32[2,1,1024]{2,1,0:T(1,128)S(1)} %get-tuple-element.39), channel_id=1, source_target_pairs={{1,0},{2,1},{3,2},{4,3},{5,4},{6,5},{7,6},{8,7},{9,8},{10,9},{11,1... | collective-permute-start | bytes 24584 | tf_op jit(solution)/shard_map/ppermute | solution.py:23
where the time goes:
time: 271 us
  blocking collectives  190 us (70%)
  starting transfers between devices  23.8 us (9%)
  waiting for transfers between devices  22.2 us (8%)
  other arithmetic  21.9 us (8%)
  between operations  7.55 us (3%)
  local copies, waits for them, and re-layouts  5.13 us (2%)
    psum x3, blocking collectives, residual_squares(): return lax.psum(local_products(residual, residual), 'lon')  92.5 us
    psum x2, blocking collectives, on_device(): step_size = norm_now / lax.psum(local_products(direction, image_vec), 'lon')  67.8 us
    psum x1, blocking collectives, on_device(): lax.psum((local_inner(first_tracer, first_surface, first_tracer, first_su...  30 us
    ppermute x5, starting transfers between devices, extended_2(): lax.ppermute(lax.slice_in_dim(block, 0, width, axis=dim), axis, backward)  16.5 us
    ppermute x5, waiting for transfers between devices, extended_2(): lax.ppermute(lax.slice_in_dim(block, block.shape[dim] - width, None, axis...  12.4 us
    ppermute x5, waiting for transfers between devices, extended_2(): lax.ppermute(lax.slice_in_dim(block, 0, width, axis=dim), axis, backward)  9.78 us
    ppermute x5, starting transfers between devices, extended_2(): lax.ppermute(lax.slice_in_dim(block, block.shape[dim] - width, None, axis...  7.28 us
  transfers between devices with their start and end apart: 10, of which 7 were waited for; matrix products, arithmetic and copies ran while one was open for 1% of the time, Pallas kernels for 0%

commit v1 on v0

--- a/solution.py
+++ b/solution.py
@@ -114,7 +114,9 @@
     norm_now = residual_squares(residual)
     for iteration in range(ITERS):
         image_vec = apply_operator(direction, face_x, face_y)
-        step_size = norm_now / lax.psum(local_products(direction, image_vec), "lon")
+        step_size = norm_now / jnp.sum(
+            lax.all_gather(local_products(direction, image_vec), "lon"), axis=0
+        )
         solution = solution + step_size[:, None, None] * direction
         residual = residual - step_size[:, None, None] * image_vec
         if iteration + 1 < ITERS:

time: 271 us -> 273 us (level)
  local copies, waits for them, and re-layouts: 5.13 us -> 9.85 us
  waiting for transfers between devices: 22.2 us -> 18.6 us
    unnamed x0 -> x2, blocking collectives: none -> 67.8 us
    psum x2 -> x0, blocking collectives: 67.8 us -> none  [on_device(): step_size = norm_now / lax.psum(local_products(direction, image_vec), 'lon')]
  transfers between devices with their start and end apart: 10 -> 10, of which waited for: 7 -> 6; matrix products, arithmetic and copies ran while one was open for 1% -> 2% of each run, Pallas kernels for 0% -> 0%
where the time goes in v1:
time: 273 us
  blocking collectives  191 us (70%)
  starting transfers between devices  23.6 us (9%)
  other arithmetic  22 us (8%)
  waiting for transfers between devices  18.6 us (7%)
  local copies, waits for them, and re-layouts  9.85 us (4%)
  between operations  8.22 us (3%)
    psum x3, blocking collectives, residual_squares(): return lax.psum(local_products(residual, residual), 'lon')  92.8 us
    unnamed x2, blocking collectives  67.8 us
    psum x1, blocking collectives, on_device(): lax.psum((local_inner(first_tracer, first_surface, first_tracer, first_su...  30 us
    ppermute x5, starting transfers between devices, extended_2(): lax.ppermute(lax.slice_in_dim(block, 0, width, axis=dim), axis, backward)  16.3 us
    ppermute x5, waiting for transfers between devices, extended_2(): lax.ppermute(lax.slice_in_dim(block, block.shape[dim] - width, None, axis...  11.1 us
    ppermute x5, waiting for transfers between devices, extended_2(): lax.ppermute(lax.slice_in_dim(block, 0, width, axis=dim), axis, backward)  7.49 us
    ppermute x5, starting transfers between devices, extended_2(): lax.ppermute(lax.slice_in_dim(block, block.shape[dim] - width, None, axis...  7.3 us
  transfers between devices with their start and end apart: 10, of which 6 were waited for; matrix products, arithmetic and copies ran while one was open for 2% of the time, Pallas kernels for 0%

profile of v1, /device:TPU:0, one launch (start us, length us, event | category | flops | bytes accessed | tf_op | source)
XLA Modules:
  0.0 272.8 jit_solution(280202211000675928)
XLA Ops:
  1.5 1.6 broadcast_multiply_fusion
  5.6 5.5 %collective-permute-start.1 = (f32[203,1,1024]{2,0,1:T(8,128)S(1)}, f32[203,1,1024]{2,0,1:T(8,128)}, u32[]{:S(2)}, u32[]{:S(2)}) collective-permute-start(f32[203,1,1024]{2,0,1:T(8,128)S(1)} %copy.20), channel_id=1, source_target_pairs={{1,0},{2,1},{3,2},{4,3},{5,4},{6,5},{7,6},{8,7},{9,8},{10,9},{11,1... | collective-permute-start | bytes 2494472 | tf_op jit(solution)/shard_map/ppermute | solution.py:23
  14.0 7.3 %collective-permute-done.1 = f32[203,1,1024]{2,0,1:T(8,128)} collective-permute-done((f32[203,1,1024]{2,0,1:T(8,128)S(1)}, f32[203,1,1024]{2,0,1:T(8,128)}, u32[]{:S(2)}, u32[]{:S(2)}) %collective-permute-start.1) | collective-permute-done | bytes 831520 | tf_op jit(solution)/shard_map/ppermute | solution.py:23
  21.4 2.0 copy.22
  23.4 4.1 %collective-permute-done = f32[203,1,1024]{2,0,1:T(8,128)} collective-permute-done((f32[203,1,1024]{2,0,1:T(8,128)}, f32[203,1,1024]{2,0,1:T(8,128)}, u32[]{:S(2)}, u32[]{:S(2)}) %collective-permute-start) | collective-permute-done | bytes 831520 | tf_op jit(solution)/shard_map/ppermute | solution.py:20
  27.5 2.0 copy.21
  31.1 2.6 pad_maximum_fusion
  33.9 1.5 subtract_multiply_fusion.3
  36.3 1.5 fusion.5
  38.4 3.0 %collective-permute-start.2 = (f32[2,50,1,1024]{3,2,1,0:T(1,128)S(1)}, f32[2,50,1,1024]{3,2,1,0:T(1,128)S(1)}, u32[]{:S(2)}, u32[]{:S(2)}) collective-permute-start(f32[2,50,1,1024]{3,2,1,0:T(1,128)S(1)} %get-tuple-element.36), channel_id=1, source_target_pairs={{0,1},{1,2},{2,3},{3,4},{4,5},{5,6},{6,7},{7,8},{8,9},{9,10},{10,1... | collective-permute-start | bytes 1228808 | tf_op jit(solution)/shard_map/ppermute | solution.py:20
  41.5 1.5 collective-permute-start.3
  44.1 4.5 %collective-permute-done.2 = f32[2,50,1,1024]{3,2,1,0:T(1,128)S(1)} collective-permute-done((f32[2,50,1,1024]{3,2,1,0:T(1,128)S(1)}, f32[2,50,1,1024]{3,2,1,0:T(1,128)S(1)}, u32[]{:S(2)}, u32[]{:S(2)}) %collective-permute-start.2) | collective-permute-done | bytes 409632 | tf_op jit(solution)/shard_map/ppermute | solution.py:20
  48.7 1.7 subtract_multiply_fusion
  50.4 1.5 fusion.33
  52.2 4.2 %collective-permute-start.5 = (f32[2,1,1024]{2,1,0:T(1,128)S(1)}, f32[2,1,1024]{2,1,0:T(1,128)S(1)}, u32[]{:S(2)}, u32[]{:S(2)}) collective-permute-start(f32[2,1,1024]{2,1,0:T(1,128)S(1)} %get-tuple-element.42), channel_id=1, source_target_pairs={{0,1},{1,2},{2,3},{3,4},{4,5},{5,6},{6,7},{7,8},{8,9},{9,10},{10,1... | collective-permute-start | bytes 24584 | tf_op jit(solution)/shard_map/ppermute | solution.py:20
  58.6 33.9 %all-reduce.10 = (f32[2]{0:T(128)S(1)}, f32[32]{0:T(128)S(1)}) all-reduce(f32[2]{0:T(128)S(1)} %get-tuple-element.13, f32[32]{0:T(128)S(1)} %dynamic-update-slice), channel_id=1, replica_groups=mesh['grp'=2,'lon'=16] {'lon'}, use_global_device_ids=true, to_apply=%region_3.4 | all-reduce | flops 34 | bytes 272 | tf_op jit(solution)/shard_map/psum | solution.py:71
  92.7 29.5 %psum.43 = f32[2]{0:T(128)S(1)} all-reduce(f32[2]{0:T(128)S(1)} %get-tuple-element.27), channel_id=1, replica_groups=mesh['grp'=2,'lon'=16] {'lon'}, use_global_device_ids=true, to_apply=%region_7.8 | all-reduce | flops 2 | bytes 16 | tf_op jit(solution)/shard_map/psum | solution.py:71
  122.4 4.4 %collective-permute-start.6 = (f32[2,1,1024]{2,1,0:T(1,128)S(1)}, f32[2,1,1024]{2,1,0:T(1,128)S(1)}, u32[]{:S(2)}, u32[]{:S(2)}) collective-permute-start(f32[2,1,1024]{2,1,0:T(1,128)S(1)} %get-tuple-element.41), channel_id=1, source_target_pairs={{1,0},{2,1},{3,2},{4,3},{5,4},{6,5},{7,6},{8,7},{9,8},{10,9},{11,1... | collective-permute-start | bytes 24584 | tf_op jit(solution)/shard_map/ppermute | solution.py:23
  128.6 33.9 %all-reduce.7 = f32[32]{0:T(128)S(1)} all-reduce(f32[32]{0:T(128)S(1)} %dynamic-update-slice.1), channel_id=3, replica_groups=mesh['grp'=2,'lon'=16] {'lon'}, use_global_device_ids=true, to_apply=%add.7 | all-reduce | flops 32 | bytes 256
  162.8 29.5 %psum.44 = f32[2]{0:T(128)S(1)} all-reduce(f32[2]{0:T(128)S(1)} %get-tuple-element.23), channel_id=1, replica_groups=mesh['grp'=2,'lon'=16] {'lon'}, use_global_device_ids=true, to_apply=%region_11.12 | all-reduce | flops 2 | bytes 16 | tf_op jit(solution)/shard_map/psum | solution.py:71
  192.4 4.4 %collective-permute-start.8 = (f32[2,1,1024]{2,1,0:T(1,128)S(1)}, f32[2,1,1024]{2,1,0:T(1,128)S(1)}, u32[]{:S(2)}, u32[]{:S(2)}) collective-permute-start(f32[2,1,1024]{2,1,0:T(1,128)S(1)} %get-tuple-element.39), channel_id=1, source_target_pairs={{1,0},{2,1},{3,2},{4,3},{5,4},{6,5},{7,6},{8,7},{9,8},{10,9},{11,1... | collective-permute-start | bytes 24584 | tf_op jit(solution)/shard_map/ppermute | solution.py:23
  198.7 33.9 %all-reduce.8 = f32[32]{0:T(128)S(1)} all-reduce(f32[32]{0:T(128)S(1)} %dynamic-update-slice.2), channel_id=4, replica_groups=mesh['grp'=2,'lon'=16] {'lon'}, use_global_device_ids=true, to_apply=%add.8 | all-reduce | flops 32 | bytes 256
  237.3 30.0 %all-reduce.9 = (f32[]{:T(128)}, f32[]{:T(128)}, f32[]{:T(128)}) all-reduce(f32[]{:T(128)S(6)} %div.73, f32[]{:T(128)S(6)} %div.78, f32[]{:T(128)S(6)} %div.76), channel_id=1, replica_groups=mesh['grp'=2,'lon'=16] {'lon'}, use_global_device_ids=true, to_apply=%region_15.16 | all-reduce | flops 3 | bytes 24 | tf_op jit(solution)/shard_map/psum | solution.py:133
  270.9 1.3 pad_maximum_fusion.3
  (87 shorter events, 19.3 us)
Async XLA Ops:
  1.5 1.7 copy-start.3
  1.5 1.7 copy-start.1
  3.1 1.0 copy-start
  3.1 1.1 copy-start.2
  5.5 6.8 %copy-start.4 = (u32[32]{0:T(128)S(1)}, u32[32]{0:T(128)}, u32[]{:S(2)}) copy-start(u32[32]{0:T(128)} %constant.49) | copy-start | bytes 388
  5.6 15.7 %collective-permute-start.1 = (f32[203,1,1024]{2,0,1:T(8,128)S(1)}, f32[203,1,1024]{2,0,1:T(8,128)}, u32[]{:S(2)}, u32[]{:S(2)}) collective-permute-start(f32[203,1,1024]{2,0,1:T(8,128)S(1)} %copy.20), channel_id=1, source_target_pairs={{1,0},{2,1},{3,2},{4,3},{5,4},{6,5},{7,6},{8,7},{9,8},{10,9},{11,1... | collective-permute-start | bytes 2494472 | tf_op jit(solution)/shard_map/ppermute | solution.py:23
  12.2 15.2 %collective-permute-start = (f32[203,1,1024]{2,0,1:T(8,128)}, f32[203,1,1024]{2,0,1:T(8,128)}, u32[]{:S(2)}, u32[]{:S(2)}) collective-permute-start(f32[203,1,1024]{2,0,1:T(8,128)} %copy.19), channel_id=1, source_target_pairs={{0,1},{1,2},{2,3},{3,4},{4,5},{5,6},{6,7},{7,8},{8,9},{9,10},{10,1... | collective-permute-start | bytes 2494472 | tf_op jit(solution)/shard_map/ppermute | solution.py:20
  38.4 10.2 %collective-permute-start.2 = (f32[2,50,1,1024]{3,2,1,0:T(1,128)S(1)}, f32[2,50,1,1024]{3,2,1,0:T(1,128)S(1)}, u32[]{:S(2)}, u32[]{:S(2)}) collective-permute-start(f32[2,50,1,1024]{3,2,1,0:T(1,128)S(1)} %get-tuple-element.36), channel_id=1, source_target_pairs={{0,1},{1,2},{2,3},{3,4},{4,5},{5,6},{6,7},{7,8},{8,9},{9,10},{10,1... | collective-permute-start | bytes 1228808 | tf_op jit(solution)/shard_map/ppermute | solution.py:20
  41.5 7.2 %collective-permute-start.3 = (f32[2,50,1,1024]{3,2,1,0:T(1,128)S(1)}, f32[2,50,1,1024]{3,2,1,0:T(1,128)S(1)}, u32[]{:S(2)}, u32[]{:S(2)}) collective-permute-start(f32[2,50,1,1024]{3,2,1,0:T(1,128)S(1)} %get-tuple-element.37), channel_id=1, source_target_pairs={{1,0},{2,1},{3,2},{4,3},{5,4},{6,5},{7,6},{8,7},{9,8},{10,9},{11,1... | collective-permute-start | bytes 1228808 | tf_op jit(solution)/shard_map/ppermute | solution.py:23
  52.2 5.8 %collective-permute-start.5 = (f32[2,1,1024]{2,1,0:T(1,128)S(1)}, f32[2,1,1024]{2,1,0:T(1,128)S(1)}, u32[]{:S(2)}, u32[]{:S(2)}) collective-permute-start(f32[2,1,1024]{2,1,0:T(1,128)S(1)} %get-tuple-element.42), channel_id=1, source_target_pairs={{0,1},{1,2},{2,3},{3,4},{4,5},{5,6},{6,7},{7,8},{8,9},{9,10},{10,1... | collective-permute-start | bytes 24584 | tf_op jit(solution)/shard_map/ppermute | solution.py:20
  56.3 1.8 collective-permute-start.4
  122.3 5.8 %collective-permute-start.7 = (f32[2,1,1024]{2,1,0:T(1,128)S(1)}, f32[2,1,1024]{2,1,0:T(1,128)S(1)}, u32[]{:S(2)}, u32[]{:S(2)}) collective-permute-start(f32[2,1,1024]{2,1,0:T(1,128)S(1)} %get-tuple-element.40), channel_id=1, source_target_pairs={{0,1},{1,2},{2,3},{3,4},{4,5},{5,6},{6,7},{7,8},{8,9},{9,10},{10,1... | collective-permute-start | bytes 24584 | tf_op jit(solution)/shard_map/ppermute | solution.py:20
  122.4 5.8 %collective-permute-start.6 = (f32[2,1,1024]{2,1,0:T(1,128)S(1)}, f32[2,1,1024]{2,1,0:T(1,128)S(1)}, u32[]{:S(2)}, u32[]{:S(2)}) collective-permute-start(f32[2,1,1024]{2,1,0:T(1,128)S(1)} %get-tuple-element.41), channel_id=1, source_target_pairs={{1,0},{2,1},{3,2},{4,3},{5,4},{6,5},{7,6},{8,7},{9,8},{10,9},{11,1... | collective-permute-start | bytes 24584 | tf_op jit(solution)/shard_map/ppermute | solution.py:23
  192.4 5.8 %collective-permute-start.9 = (f32[2,1,1024]{2,1,0:T(1,128)S(1)}, f32[2,1,1024]{2,1,0:T(1,128)S(1)}, u32[]{:S(2)}, u32[]{:S(2)}) collective-permute-start(f32[2,1,1024]{2,1,0:T(1,128)S(1)} %get-tuple-element.38), channel_id=1, source_target_pairs={{0,1},{1,2},{2,3},{3,4},{4,5},{5,6},{6,7},{7,8},{8,9},{9,10},{10,1... | collective-permute-start | bytes 24584 | tf_op jit(solution)/shard_map/ppermute | solution.py:20
  192.4 5.8 %collective-permute-start.8 = (f32[2,1,1024]{2,1,0:T(1,128)S(1)}, f32[2,1,1024]{2,1,0:T(1,128)S(1)}, u32[]{:S(2)}, u32[]{:S(2)}) collective-permute-start(f32[2,1,1024]{2,1,0:T(1,128)S(1)} %get-tuple-element.39), channel_id=1, source_target_pairs={{1,0},{2,1},{3,2},{4,3},{5,4},{6,5},{7,6},{8,7},{9,8},{10,9},{11,1... | collective-permute-start | bytes 24584 | tf_op jit(solution)/shard_map/ppermute | solution.py:23
